TPU v7x, 512 devices: a whole 4x4x16 slice. The times are simulated.
512 devices in a mesh: sx: 32 (over z_hi, y, core), sy: 16 (over x, z_lo).
Axes of the slice: x: 4, y: 4, z: 16 (z_hi: 4, z_lo: 4; z = z_hi * 4 + z_lo), core: 2. Of those that a mesh axis runs over, the one named last changes fastest.
Arguments:
- forward_prop: bfloat16 [2, 2, 12, 12, 64, 4096], P(None, None, None, None, 'sx', 'sy'), may hold values from -0.08984375 to 0.08984375
- backward_prop: bfloat16 [2, 2, 12, 12, 64, 4096], P(None, None, None, None, 'sx', 'sy'), may hold values from -0.08984375 to 0.08984375
- gamma_table: int32 [16, 4, 2], replicated, may hold values from 0 to 3, as said below
- source_site: int32 [3], replicated, may hold values from 0 to 63
- momenta: int32 [32, 3], replicated, may hold values from -8 to 7
Outputs:
- corr: float32 [16, 2, 2, 64, 4096], P(None, None, None, 'sx', 'sy')
- listed: float32 [2, 16, 2, 32], replicated
Inputs may be any that keep to these rules, and one draw needn't show every extreme that they name: For every insertion g, gamma_table[g, 0..3, 0] is a permutation of 0..3; gamma_table[g, s, 1] is the power of i of that entry.
All inputs are finite; a program needn't handle non-finite values.
Results may differ from a plain program's by a relative error of at most 0.0003.
Values sent between devices are 32-bit elements; how exact they have to be, the bound alone decides.
A program may use at most 64 MiB of HBM per device.

v0:
```python
import math
import jax
import jax.numpy as jnp
from jax import lax
from jax.sharding import PartitionSpec as P

L = 64
LZ = 64
HIGHEST = lax.Precision.HIGHEST


def gamma_matrices(gamma_table):
    inserts = gamma_table.shape[0]
    columns = gamma_table[:, :, 0]
    powers = gamma_table[:, :, 1]
    spin_ids = jnp.arange(4, dtype=jnp.int32)
    matches = (columns[:, :, None] == spin_ids[None, None, :]).astype(jnp.float32)
    unit_re = (powers == 0).astype(jnp.float32) - (powers == 2).astype(jnp.float32)
    unit_im = (powers == 1).astype(jnp.float32) - (powers == 3).astype(jnp.float32)
    return (
        (matches * unit_re[:, :, None]).reshape(inserts, 16),
        (matches * unit_im[:, :, None]).reshape(inserts, 16),
    )


def dft_table(length, anchor):
    wavenum = jnp.arange(length, dtype=jnp.int32)
    offsets = jnp.mod(wavenum - anchor, length)
    phase_index = jnp.mod(offsets[:, None] * wavenum[None, :], length)
    angles = 2.0 * math.pi / length * phase_index.astype(jnp.float32)
    return (jnp.cos(angles), -jnp.sin(angles))


def complex_step(real_part, imag_part, table_re, table_im, pattern):
    out_re = jnp.einsum(pattern, real_part, table_re, precision=HIGHEST) - jnp.einsum(
        pattern, imag_part, table_im, precision=HIGHEST
    )
    out_im = jnp.einsum(pattern, real_part, table_im, precision=HIGHEST) + jnp.einsum(
        pattern, imag_part, table_re, precision=HIGHEST
    )
    return (out_re, out_im)


def transform(fields, source_site):
    table_re, table_im = dft_table(fields.shape[4], source_site[2])
    along_z = jnp.stack(
        complex_step(fields[:, 0], fields[:, 1], table_re, table_im, "nabz,zk->nabk"), 1
    )
    depth_share = along_z.shape[4] // lax.axis_size("sy")
    first_depth = lax.axis_index("sy") * depth_share
    length_y = along_z.shape[3] * lax.axis_size("sy")
    full_re, full_im = dft_table(length_y, source_site[1])
    part = lax.dynamic_slice_in_dim(
        lax.all_gather(along_z, "sy", axis=3, tiled=True), first_depth, depth_share, 4
    )
    step_re, step_im = complex_step(part[:, 0], part[:, 1], full_re, full_im, "nayc,yk->nakc")
    along_y = jnp.stack([step_re, step_im], 1)
    arrived = lax.all_to_all(along_y, "sx", split_axis=3, concat_axis=2, tiled=True)
    table_re, table_im = dft_table(arrived.shape[2], source_site[0])
    along_x = complex_step(arrived[:, 0], arrived[:, 1], table_re, table_im, "nxbc,xk->nbck")
    return jnp.stack(along_x, 1)


def apply_gammas(mat_re, mat_im, real_part, imag_part):
    extent = real_part.shape
    flat_re = real_part.reshape(extent[0], -1)
    flat_im = imag_part.reshape(extent[0], -1)
    out_re = jnp.dot(mat_re, flat_re, precision=HIGHEST) - jnp.dot(
        mat_im, flat_im, precision=HIGHEST
    )
    out_im = jnp.dot(mat_re, flat_im, precision=HIGHEST) + jnp.dot(
        mat_im, flat_re, precision=HIGHEST
    )
    return (out_re.reshape(extent), out_im.reshape(extent))


def project_sites(fields, source_site, momenta, rows_x, rows_y, length, depth):
    coord_x = lax.axis_index("sx") * rows_x + jnp.arange(rows_x, dtype=jnp.int32) - source_site[0]
    coord_y = lax.axis_index("sy") * rows_y + jnp.arange(rows_y, dtype=jnp.int32) - source_site[1]
    coord_z = jnp.arange(depth, dtype=jnp.int32) - source_site[2]
    part_x = jnp.mod(momenta[:, 0:1] * coord_x[None, :], length)
    part_y = jnp.mod(momenta[:, 1:2] * coord_y[None, :], length)
    part_z = jnp.mod(momenta[:, 2:3] * coord_z[None, :], depth)
    plane = jnp.mod(part_x[:, :, None] + part_y[:, None, :], length).astype(jnp.float32)
    angles = (
        2.0 * math.pi / length * plane[:, :, :, None]
        + 2.0 * math.pi / depth * part_z.astype(jnp.float32)[:, None, None, :]
    )
    angles = angles.reshape(momenta.shape[0], -1)
    cosine = jnp.cos(angles)
    sine = jnp.sin(angles)
    field_re = fields[:, 0].reshape(fields.shape[0], -1)
    field_im = fields[:, 1].reshape(fields.shape[0], -1)
    local_re = jnp.dot(field_re, cosine.T, precision=HIGHEST) + jnp.dot(
        field_im, sine.T, precision=HIGHEST
    )
    local_im = jnp.dot(field_im, cosine.T, precision=HIGHEST) - jnp.dot(
        field_re, sine.T, precision=HIGHEST
    )
    return (local_re, local_im)


def body(forward_prop, backward_prop, gamma_table, source_site, momenta):
    slices = forward_prop.shape[0]
    rows_x = forward_prop.shape[4]
    rows_y = backward_prop.shape[5] // LZ
    inserts = gamma_table.shape[0]
    forward = forward_prop.reshape(slices, 2, 4, 3, 12, -1)
    backward = backward_prop.reshape(slices, 2, 4, 3, 12, -1)
    pattern = "tscjn,tucjn->sutn"
    pair_re = jnp.einsum(
        pattern, backward[:, 0], forward[:, 0], preferred_element_type=jnp.float32
    ) + jnp.einsum(pattern, backward[:, 1], forward[:, 1], preferred_element_type=jnp.float32)
    pair_im = jnp.einsum(
        pattern, backward[:, 0], forward[:, 1], preferred_element_type=jnp.float32
    ) - jnp.einsum(pattern, backward[:, 1], forward[:, 0], preferred_element_type=jnp.float32)
    pair_re = pair_re.reshape(16, slices, -1)
    pair_im = pair_im.reshape(16, slices, -1)
    mat_re, mat_im = gamma_matrices(gamma_table)
    field_re, field_im = apply_gammas(mat_re, mat_im, pair_re, pair_im)
    fields = jnp.stack([field_re, field_im], 2).reshape(inserts * slices, 2, rows_x, rows_y, LZ)
    spectrum = transform(fields, source_site)
    local_re, local_im = project_sites(fields, source_site, momenta, rows_x, rows_y, L, LZ)
    listed_re, listed_im = lax.psum((local_re, local_im), ("sx", "sy"))
    listed_re = listed_re.reshape(inserts, slices, -1)
    listed_im = listed_im.reshape(inserts, slices, -1)
    corr_re = spectrum[:, 0].reshape(inserts, slices, spectrum.shape[2], -1)
    corr_im = spectrum[:, 1].reshape(inserts, slices, spectrum.shape[2], -1)
    return (jnp.stack([corr_re, corr_im], 2), jnp.stack([listed_re, listed_im], 0))


def solution(mesh):
    placed = (
        P(None, None, None, None, "sx", "sy"),
        P(None, None, None, None, "sx", "sy"),
        P(),
        P(),
        P(),
    )
    return jax.shard_map(
        body,
        mesh=mesh,
        in_specs=placed,
        out_specs=(P(None, None, None, "sx", "sy"), P()),
        check_vma=False,
    )
```

profile of v0, /device:TPU:1, one launch (start us, length us, event | category | flops | bytes accessed | tf_op | source)
XLA Modules:
  0.0 323.4 jit_solution(12954592644119887692)
XLA Ops:
  7.2 0.7 fusion.92
  7.9 2.1 reshape.371
  10.0 0.8 fusion.144
  10.9 4.5 %copy.82 = bf16[2,1,4,3,12,512]{4,2,3,5,0,1:T(4,128)(2,1)S(1)} copy(bf16[2,1,4,3,12,512]{5,4,3,2,1,0:T(8,128)(2,1)} %get-tuple-element.11) | data formatting | bytes 589824
  15.3 2.8 reshape.372
  18.1 2.1 fusion.145
  20.2 5.3 %copy.83 = bf16[2,1,4,3,12,512]{4,2,3,5,0,1:T(4,128)(2,1)} copy(bf16[2,1,4,3,12,512]{5,4,3,2,1,0:T(8,128)(2,1)} %get-tuple-element.13) | data formatting | bytes 589824
  25.4 3.8 %copy.80 = bf16[2,1,4,3,12,512]{4,2,3,5,0,1:T(4,128)(2,1)} copy(bf16[2,1,4,3,12,512]{5,4,3,2,1,0:T(8,128)(2,1)S(1)} %get-tuple-element.10) | data formatting | bytes 589824
  29.2 5.3 %copy.81 = bf16[2,1,4,3,12,512]{4,2,3,5,0,1:T(4,128)(2,1)} copy(bf16[2,1,4,3,12,512]{5,4,3,2,1,0:T(8,128)(2,1)} %get-tuple-element.12) | data formatting | bytes 589824
  34.5 5.6 %fusion.2 = f32[2,512,4,4,1]{3,2,4,1,0:T(4,128)S(1)} fusion(bf16[2,1,4,3,12,512]{4,2,3,5,0,1:T(4,128)(2,1)} %copy.83, bf16[2,1,4,3,12,512]{4,2,3,5,0,1:T(4,128)(2,1)S(1)} %copy.82), kind=kOutput, calls=%fused_computation.2 | convolution fusion | flops 1179648 | bytes 655360 | tf_op jit(solution)/shard_map/tscjn,tucjn->sutn/dot_general | solution.py:113
  40.2 5.0 %fusion = f32[2,512,4,4,1]{3,2,4,1,0:T(4,128)} fusion(bf16[2,1,4,3,12,512]{4,2,3,5,0,1:T(4,128)(2,1)S(1)} %copy-done.1, bf16[2,1,4,3,12,512]{4,2,3,5,0,1:T(4,128)(2,1)S(1)} %copy-done.2), kind=kOutput, calls=%fused_computation | convolution fusion | flops 1179648 | bytes 655360 | tf_op jit(solution)/shard_map/tscjn,tucjn->sutn/dot_general | solution.py:116
  45.2 3.7 %fusion.13 = f32[4,4,2,512]{0,1,3,2:T(4,128)} fusion(f32[2,512,4,4,1]{3,2,4,1,0:T(4,128)S(1)} %fusion.2, bf16[2,1,4,3,12,512]{4,2,3,5,0,1:T(4,128)(2,1)S(1)} %copy-done, bf16[2,1,4,3,12,512]{4,2,3,5,0,1:T(4,128)(2,1)S(1)} %copy-done.2), kind=kOutput, calls=%fused_computation.17 | convolution fusion | flops 1196032 | bytes 720896 | tf_op jit(solution)/shard_map/tscjn,tucjn->sutn/dot_general | solution.py:111
  48.8 2.1 copy.48
  51.0 7.5 %fusion.12 = f32[4,4,2,512]{0,1,3,2:T(4,128)} fusion(f32[2,512,4,4,1]{3,2,4,1,0:T(4,128)} %fusion, bf16[2,1,4,3,12,512]{4,2,3,5,0,1:T(4,128)(2,1)} %copy.81, bf16[2,1,4,3,12,512]{4,2,3,5,0,1:T(4,128)(2,1)S(1)} %copy.82), kind=kOutput, calls=%fused_computation.15 | convolution fusion | flops 1196032 | bytes 720896 | tf_op jit(solution)/shard_map/tscjn,tucjn->sutn/dot_general | solution.py:114
  58.5 1.9 copy.49
  60.5 0.7 fusion.146
  61.1 0.3 fusion.147
  61.4 0.3 fusion.148
  61.6 0.3 convolution_subtract_fusion.3
  61.9 0.1 squeeze.52
  62.0 1.3 and_select_fusion.1
  63.3 0.5 fusion.32
  63.8 0.5 fusion.30
  64.2 0.3 convolution_add_fusion.3
  64.5 0.1 squeeze.54
  64.6 0.5 fusion.25
  65.1 0.5 fusion.24
  65.5 0.7 pad_maximum_fusion
  66.3 0.6 iota_subtract_fusion
  67.0 0.7 add_subtract_fusion.1
  67.6 0.7 add_subtract_fusion
  68.6 0.1 fusion.45
  68.7 1.1 add_sine_fusion
  69.8 0.1 cos.29
  70.0 0.7 and_select_fusion.3
  70.7 0.2 fusion.149
  70.9 0.2 convolution_add_fusion.4
  71.1 107.5 %all-gather.2.cloned.1.call-done = f32[32,2,2,64,64]{4,0,3,2,1:T(8,128)} async-done(((f32[32,2,2,4,64]{4,0,3,2,1:T(8,128)}), f32[32,2,2,64,64]{4,0,3,2,1:T(8,128)}) %all-gather.2.cloned.1.call-update) | async-done | bytes 2097168 | tf_op jit(solution)/shard_map/all_gather | solution.py:54
  178.6 4.7 %dynamic-slice_bitcast_fusion = (f32[32,2,64,4]{3,0,2,1:T(8,128)S(1)}, f32[32,2,64,4]{3,0,2,1:T(8,128)}) fusion(f32[32,2,2,64,64]{4,0,3,2,1:T(8,128)} %all-gather.2.cloned.1.call-done, s32[]{:T(128)S(6)} %add.213, s32[]{:T(128)S(6)} %select_n.88), kind=kLoop, calls=%fused_computation.12 | loop fusion | bytes 262152 | tf_op jit(solution)/shard_map/squeeze | solution.py:56
  183.3 2.6 copy.54
  186.0 0.5 fusion.51
  186.4 0.5 fusion.53
  186.9 1.2 copy.55
  188.1 0.5 fusion.23
  188.5 0.5 fusion.22
  189.0 0.3 copy.58
  189.4 1.0 reshape.373
  190.4 13.0 %all-to-all-start = ((f32[32,1,1024]{2,1,0:T(1,128)}), f32[32,1,1024]{2,1,0:T(1,128)S(1)}, u32[]{:S(2)}, u32[]{:S(2)}) async-start(f32[32,1,1024]{2,1,0:T(1,128)} %reshape.373), calls=%async_computation | async-start | bytes 262144 | tf_op jit(solution)/shard_map/all_to_all | solution.py:58
  203.4 0.2 fusion.150
  203.6 0.2 convolution_subtract_fusion.4
  203.8 106.2 %all-reduce = (f32[1,16,2,32]{3,2,1,0:T(2,128)S(1)}, f32[1,16,2,32]{3,2,1,0:T(2,128)S(1)}) all-reduce(f32[1,16,2,32]{3,2,1,0:T(2,128)S(1)} %bitcast.184, f32[1,16,2,32]{3,2,1,0:T(2,128)S(1)} %bitcast.183), channel_id=1, replica_groups=mesh['sx'=32,'sy'=16] {'sx','sy'}, use_global_device_ids=true, to_apply=%region_1.2 | all-reduce | flops 2048 | bytes 16384 | tf_op jit(solution)/shard_map/psum | solution.py:124
  309.9 0.6 pad_maximum_fusion.3
  310.6 0.5 broadcast.522
  311.1 0.9 reduce
  312.0 0.3 reshape.374
  312.3 0.2 copy.59
  312.5 0.4 copy.60
  312.9 0.6 fusion.27
  313.5 0.6 fusion.26
  314.1 0.6 convolution_subtract_fusion.2
  314.9 0.1 stack_reshape_squeeze_stack.6
  315.0 0.6 convolution_add_fusion.2
  315.7 0.1 stack_reshape_squeeze_stack.7
  315.9 0.7 copy.65
  (29 shorter events, 0.8 us)
Async XLA Ops:
  7.2 171.4 %all-gather.2.cloned.1.call-start = ((), (), s32[]{:S(2)}) async-start(), calls=%async_computation.1 | async-start | bytes 4456448 | tf_op jit(solution)/shard_map/all_gather | solution.py:54
  34.5 5.6 %copy-start.1 = (bf16[2,1,4,3,12,512]{4,2,3,5,0,1:T(4,128)(2,1)S(1)}, bf16[2,1,4,3,12,512]{4,2,3,5,0,1:T(4,128)(2,1)}, u32[]{:S(2)}) copy-start(bf16[2,1,4,3,12,512]{4,2,3,5,0,1:T(4,128)(2,1)} %copy.83) | copy-start | bytes 884740
  34.5 5.6 %copy-start.2 = (bf16[2,1,4,3,12,512]{4,2,3,5,0,1:T(4,128)(2,1)S(1)}, bf16[2,1,4,3,12,512]{4,2,3,5,0,1:T(4,128)(2,1)}, u32[]{:S(2)}) copy-start(bf16[2,1,4,3,12,512]{4,2,3,5,0,1:T(4,128)(2,1)} %copy.80) | copy-start | bytes 884740
  40.2 5.0 %copy-start = (bf16[2,1,4,3,12,512]{4,2,3,5,0,1:T(4,128)(2,1)S(1)}, bf16[2,1,4,3,12,512]{4,2,3,5,0,1:T(4,128)(2,1)}, u32[]{:S(2)}) copy-start(bf16[2,1,4,3,12,512]{4,2,3,5,0,1:T(4,128)(2,1)} %copy.81) | copy-start | bytes 884740
  50.9 9.5 %copy-start.3 = (s32[3]{0:T(128)S(1)}, s32[3]{0:T(128)}, u32[]{:S(2)}) copy-start(s32[3]{0:T(128)} %param.8) | copy-start | bytes 40
  50.9 10.2 %slice-start = ((s32[16,4,2]{0,2,1:T(2,128)}), s32[16,4,1]{0,2,1:T(1,128)S(1)}, s32[]{:S(2)}) async-start(s32[16,4,2]{0,2,1:T(2,128)} %param.7), calls=%async_computation.2 | async-start | bytes 4096 | tf_op jit(solution)/shard_map/slice | solution.py:14
  58.5 9.8 %copy-start.4 = (s32[32,3]{0,1:T(4,128)S(1)}, s32[32,3]{0,1:T(4,128)}, u32[]{:S(2)}) copy-start(s32[32,3]{0,1:T(4,128)} %param.9) | copy-start | bytes 1156
  190.4 120.2 %all-to-all-start = ((f32[32,1,1024]{2,1,0:T(1,128)}), f32[32,1,1024]{2,1,0:T(1,128)S(1)}, u32[]{:S(2)}, u32[]{:S(2)}) async-start(f32[32,1,1024]{2,1,0:T(1,128)} %reshape.373), calls=%async_computation | async-start | bytes 262144 | tf_op jit(solution)/shard_map/all_to_all | solution.py:58
Sparse Core Ops, SparseCore 0:
  66.4 112.1 all-gather.1
where the time goes:
time: 325 us; the launch traced here: 323 us
  waiting for transfers between devices  108 us (33%)
  blocking collectives  106 us (33%)
  local copies, waits for them, and re-layouts  44.1 us (14%)
  matrix products  29.7 us (9%)
  between operations  14.4 us (4%)
  starting transfers between devices  13 us (4%)
  other arithmetic  8.45 us (3%)
    all_gather x1, waiting for transfers between devices, transform(): lax.all_gather(along_z, 'sy', axis=3, tiled=True)  107 us
    psum x1, blocking collectives, body(): listed_re, listed_im = lax.psum((local_re, local_im), ('sx', 'sy'))  106 us
    unnamed x19, local copies, waits for them, and re-layouts  20.8 us
    all_to_all x1, starting transfers between devices, transform(): lax.all_to_all(along_y, 'sx', split_axis=3, concat_axis=2, tiled=True)  13 us
    dot_general x1, matrix products, body(): jnp.einsum(pattern, backward[:, 0], forward[:, 1], preferred_element_type...  7.53 us
  transfers between devices with their start and end apart: 2, of which 1 were waited for; matrix products, arithmetic and copies ran while one was open for 2% of the time, Pallas kernels for 0%

commit v1 on v0

--- a/solution.py
+++ b/solution.py
@@ -121,7 +121,7 @@
     fields = jnp.stack([field_re, field_im], 2).reshape(inserts * slices, 2, rows_x, rows_y, LZ)
     spectrum = transform(fields, source_site)
     local_re, local_im = project_sites(fields, source_site, momenta, rows_x, rows_y, L, LZ)
-    listed_re, listed_im = lax.psum((local_re, local_im), ("sx", "sy"))
+    listed_re, listed_im = lax.psum(lax.psum((local_re, local_im), "sx"), "sy")
     listed_re = listed_re.reshape(inserts, slices, -1)
     listed_im = listed_im.reshape(inserts, slices, -1)
     corr_re = spectrum[:, 0].reshape(inserts, slices, spectrum.shape[2], -1)

time: 325 us -> 464 us (1.43)
  the two profiles are of different devices: /device:TPU:1 before, /device:TPU:0 now
where the time goes in v1:
time: 464 us; the launch traced here: 463 us
  blocking collectives  252 us (54%)
  waiting for transfers between devices  102 us (22%)
  local copies, waits for them, and re-layouts  44.1 us (10%)
  matrix products  29.8 us (6%)
  between operations  14.4 us (3%)
  starting transfers between devices  12.4 us (3%)
  other arithmetic  8.31 us (2%)
    psum x2, blocking collectives, body(): listed_re, listed_im = lax.psum(lax.psum((local_re, local_im), 'sx'), 'sy')  252 us
    all_gather x1, waiting for transfers between devices, transform(): lax.all_gather(along_z, 'sy', axis=3, tiled=True)  102 us
    unnamed x19, local copies, waits for them, and re-layouts  20.8 us
    all_to_all x1, starting transfers between devices, transform(): lax.all_to_all(along_y, 'sx', split_axis=3, concat_axis=2, tiled=True)  12.3 us
  transfers between devices with their start and end apart: 2, of which 1 were waited for; matrix products, arithmetic and copies ran while one was open for 1% of the time, Pallas kernels for 0%

profile of v1, /device:TPU:0, one launch (start us, length us, event | category | flops | bytes accessed | tf_op | source)
XLA Modules:
  0.0 462.9 jit_solution(12240136589755531679)
XLA Ops:
  7.2 0.7 fusion.92
  7.9 2.1 reshape.371
  10.0 0.8 fusion.144
  10.8 4.5 copy.82
  15.3 2.8 reshape.372
  18.1 2.1 fusion.145
  20.2 5.3 %copy.83 = bf16[2,1,4,3,12,512]{4,2,3,5,0,1:T(4,128)(2,1)} copy(bf16[2,1,4,3,12,512]{5,4,3,2,1,0:T(8,128)(2,1)} %get-tuple-element.15) | data formatting | bytes 589824
  25.5 3.8 copy.80
  29.3 5.3 %copy.81 = bf16[2,1,4,3,12,512]{4,2,3,5,0,1:T(4,128)(2,1)} copy(bf16[2,1,4,3,12,512]{5,4,3,2,1,0:T(8,128)(2,1)} %get-tuple-element.14) | data formatting | bytes 589824
  34.6 5.6 %fusion.2 = f32[2,512,4,4,1]{3,2,4,1,0:T(4,128)S(1)} fusion(bf16[2,1,4,3,12,512]{4,2,3,5,0,1:T(4,128)(2,1)} %copy.83, bf16[2,1,4,3,12,512]{4,2,3,5,0,1:T(4,128)(2,1)S(1)} %copy.82), kind=kOutput, calls=%fused_computation.2 | convolution fusion | flops 1179648 | bytes 655360 | tf_op jit(solution)/shard_map/tscjn,tucjn->sutn/dot_general | solution.py:113
  40.2 5.0 %fusion = f32[2,512,4,4,1]{3,2,4,1,0:T(4,128)} fusion(bf16[2,1,4,3,12,512]{4,2,3,5,0,1:T(4,128)(2,1)S(1)} %copy-done.1, bf16[2,1,4,3,12,512]{4,2,3,5,0,1:T(4,128)(2,1)S(1)} %copy-done.2), kind=kOutput, calls=%fused_computation | convolution fusion | flops 1179648 | bytes 655360 | tf_op jit(solution)/shard_map/tscjn,tucjn->sutn/dot_general | solution.py:116
  45.2 3.7 fusion.13
  48.9 2.1 copy.48
  51.0 7.5 %fusion.12 = f32[4,4,2,512]{0,1,3,2:T(4,128)} fusion(f32[2,512,4,4,1]{3,2,4,1,0:T(4,128)} %fusion, bf16[2,1,4,3,12,512]{4,2,3,5,0,1:T(4,128)(2,1)} %copy.81, bf16[2,1,4,3,12,512]{4,2,3,5,0,1:T(4,128)(2,1)S(1)} %copy.82), kind=kOutput, calls=%fused_computation.15 | convolution fusion | flops 1196032 | bytes 720896 | tf_op jit(solution)/shard_map/tscjn,tucjn->sutn/dot_general | solution.py:114
  58.6 1.9 copy.49
  60.5 0.6 fusion.146
  61.1 0.3 fusion.147
  61.4 0.3 fusion.148
  61.6 0.3 convolution_subtract_fusion.3
  61.9 0.1 squeeze.52
  62.0 1.2 and_select_fusion.1
  63.2 0.5 fusion.32
  63.7 0.5 fusion.30
  64.2 0.3 convolution_add_fusion.3
  64.4 0.1 squeeze.54
  64.5 0.5 fusion.25
  65.0 0.5 fusion.24
  65.5 0.7 pad_maximum_fusion
  66.3 0.6 iota_subtract_fusion
  66.8 0.7 add_subtract_fusion.1
  67.5 0.7 add_subtract_fusion
  68.4 0.1 fusion.45
  68.6 1.1 add_sine_fusion
  69.9 0.7 and_select_fusion.3
  70.6 0.2 fusion.149
  70.8 0.2 convolution_add_fusion.4
  71.0 101.6 %all-gather.2.cloned.1.call-done = f32[32,2,2,64,64]{4,0,3,2,1:T(8,128)} async-done(((f32[32,2,2,4,64]{4,0,3,2,1:T(8,128)}), f32[32,2,2,64,64]{4,0,3,2,1:T(8,128)}) %all-gather.2.cloned.1.call-update) | async-done | bytes 2097168 | tf_op jit(solution)/shard_map/all_gather | solution.py:54
  172.6 4.7 %dynamic-slice_bitcast_fusion = (f32[32,2,64,4]{3,0,2,1:T(8,128)S(1)}, f32[32,2,64,4]{3,0,2,1:T(8,128)}) fusion(f32[32,2,2,64,64]{4,0,3,2,1:T(8,128)} %all-gather.2.cloned.1.call-done, s32[]{:T(128)S(6)} %add.217, s32[]{:T(128)S(6)} %select_n.88), kind=kLoop, calls=%fused_computation.12 | loop fusion | bytes 262152 | tf_op jit(solution)/shard_map/squeeze | solution.py:56
  177.3 2.6 copy.54
  179.9 0.5 fusion.51
  180.4 0.5 fusion.53
  180.8 1.2 copy.55
  182.0 0.5 fusion.23
  182.5 0.5 fusion.22
  183.0 0.3 copy.58
  183.3 1.0 reshape.373
  184.3 12.3 %all-to-all-start = ((f32[32,1,1024]{2,1,0:T(1,128)}), f32[32,1,1024]{2,1,0:T(1,128)S(1)}, u32[]{:S(2)}, u32[]{:S(2)}) async-start(f32[32,1,1024]{2,1,0:T(1,128)} %reshape.373), calls=%async_computation | async-start | bytes 262144 | tf_op jit(solution)/shard_map/all_to_all | solution.py:58
  196.6 0.2 fusion.150
  196.8 0.2 convolution_subtract_fusion.4
  197.0 174.6 %all-reduce = (f32[32,32]{1,0:T(8,128)S(1)}, f32[32,32]{1,0:T(8,128)S(1)}) all-reduce(f32[32,32]{1,0:T(8,128)S(1)} %convolution_subtract_fusion.4, f32[32,32]{1,0:T(8,128)S(1)} %convolution_add_fusion.4), channel_id=1, replica_groups=mesh['sx'=32,'sy'=16] {'sx'}, use_global_device_ids=true, to_apply=%region_2.3 | all-reduce | flops 2048 | bytes 16384 | tf_op jit(solution)/shard_map/psum | solution.py:124
  371.6 77.8 %all-reduce.1 = (f32[1,16,2,32]{3,2,1,0:T(2,128)S(1)}, f32[1,16,2,32]{3,2,1,0:T(2,128)S(1)}) all-reduce(f32[1,16,2,32]{3,2,1,0:T(2,128)S(1)} %bitcast.183, f32[1,16,2,32]{3,2,1,0:T(2,128)S(1)} %bitcast.184), channel_id=1, replica_groups=mesh['sx'=32,'sy'=16] {'sy'}, use_global_device_ids=true, to_apply=%region_3.4 | all-reduce | flops 2048 | bytes 16384 | tf_op jit(solution)/shard_map/psum | solution.py:124
  449.4 0.6 pad_maximum_fusion.3
  450.1 0.5 broadcast.522
  450.6 0.9 reduce
  451.5 0.3 reshape.374
  451.8 0.2 copy.59
  452.0 0.4 copy.60
  452.4 0.6 fusion.27
  453.0 0.6 fusion.26
  453.7 0.6 convolution_subtract_fusion.2
  454.4 0.1 stack_reshape_squeeze_stack.6
  454.5 0.6 convolution_add_fusion.2
  455.2 0.1 stack_reshape_squeeze_stack.7
  455.4 0.7 copy.65
  (30 shorter events, 0.9 us)
Async XLA Ops:
  7.2 165.4 %all-gather.2.cloned.1.call-start = ((), (), s32[]{:S(2)}) async-start(), calls=%async_computation.1 | async-start | bytes 4456448 | tf_op jit(solution)/shard_map/all_gather | solution.py:54
  34.5 5.6 %copy-start.1 = (bf16[2,1,4,3,12,512]{4,2,3,5,0,1:T(4,128)(2,1)S(1)}, bf16[2,1,4,3,12,512]{4,2,3,5,0,1:T(4,128)(2,1)}, u32[]{:S(2)}) copy-start(bf16[2,1,4,3,12,512]{4,2,3,5,0,1:T(4,128)(2,1)} %copy.83) | copy-start | bytes 884740
  34.6 5.6 %copy-start.2 = (bf16[2,1,4,3,12,512]{4,2,3,5,0,1:T(4,128)(2,1)S(1)}, bf16[2,1,4,3,12,512]{4,2,3,5,0,1:T(4,128)(2,1)}, u32[]{:S(2)}) copy-start(bf16[2,1,4,3,12,512]{4,2,3,5,0,1:T(4,128)(2,1)} %copy.80) | copy-start | bytes 884740
  40.2 5.0 %copy-start = (bf16[2,1,4,3,12,512]{4,2,3,5,0,1:T(4,128)(2,1)S(1)}, bf16[2,1,4,3,12,512]{4,2,3,5,0,1:T(4,128)(2,1)}, u32[]{:S(2)}) copy-start(bf16[2,1,4,3,12,512]{4,2,3,5,0,1:T(4,128)(2,1)} %copy.81) | copy-start | bytes 884740
  51.0 9.5 %copy-start.3 = (s32[3]{0:T(128)S(1)}, s32[3]{0:T(128)}, u32[]{:S(2)}) copy-start(s32[3]{0:T(128)} %param.8) | copy-start | bytes 40
  51.0 10.1 %slice-start = ((s32[16,4,2]{0,2,1:T(2,128)}), s32[16,4,1]{0,2,1:T(1,128)S(1)}, s32[]{:S(2)}) async-start(s32[16,4,2]{0,2,1:T(2,128)} %param.7), calls=%async_computation.2 | async-start | bytes 4096 | tf_op jit(solution)/shard_map/slice | solution.py:14
  58.6 9.6 %copy-start.4 = (s32[32,3]{0,1:T(4,128)S(1)}, s32[32,3]{0,1:T(4,128)}, u32[]{:S(2)}) copy-start(s32[32,3]{0,1:T(4,128)} %param.9) | copy-start | bytes 1156
  184.3 265.8 %all-to-all-start = ((f32[32,1,1024]{2,1,0:T(1,128)}), f32[32,1,1024]{2,1,0:T(1,128)S(1)}, u32[]{:S(2)}, u32[]{:S(2)}) async-start(f32[32,1,1024]{2,1,0:T(1,128)} %reshape.373), calls=%async_computation | async-start | bytes 262144 | tf_op jit(solution)/shard_map/all_to_all | solution.py:58
Sparse Core Ops, SparseCore 0:
  66.3 106.1 all-gather.1
